TPU v7x, 32 devices: a whole 2x2x4 slice. The times are simulated.
32 devices in a mesh: dp: 4 (over y, x), segment: 2 (over core), band: 4 (over z).
Axes of the slice: x: 2, y: 2, z: 4, core: 2. Of those that a mesh axis runs over, the one named last changes fastest.
Arguments:
- fields: bfloat16 [4, 2, 32, 16, 512], P('dp', None, 'band'), may hold values from -6 to 6
- cell_mask: int32 [4, 2, 32, 16], P('dp', None, 'band'), may hold values 0 or 1
- merge_weight: bfloat16 [2, 1024, 512], P('segment', 'dp'), may hold values from -0.1875 to 0.1875
- qkv_weight: bfloat16 [2, 512, 1536], P('segment', 'dp')
- out_weight: bfloat16 [2, 512, 512], P('segment', 'dp'), may hold values from -1 to 1
- norm_gain: bfloat16 [2, 512], P('segment', 'dp'), may hold values from 0.099609375 to 1.8984375
- out_cotangent: bfloat16 [4, 2, 32, 16, 512], P('dp', None, 'band'), may hold values from -6 to 6
Outputs:
- section_out: bfloat16 [2, 4, 2, 32, 16, 512], P('segment', 'dp', None, 'band')
- merge_grad: float32 [2, 1024, 512], P('segment', 'dp')
- qkv_grad: float32 [2, 512, 1536], P('segment', 'dp')
- out_grad: float32 [2, 512, 512], P('segment', 'dp')
- gain_grad: float32 [2, 512], P('segment', 'dp')
Inputs may be any that keep to these rules, and one draw needn't show every extreme that they name: `cell_mask`: 1 marks a cell whose keys may be attended.
All inputs are finite; a program needn't handle non-finite values. No bound on the sum of `cell_mask` on one device may be relied on, other than what follows from the above.
Results may differ from a plain program's by a relative error of at most 0.03.
Values may be sent and summed in bfloat16 or wider, within the bound.
No kernel may reach another device: no remote copies, remote signals or barrier semaphores. Data moves between devices by JAX's collectives and lax.ppermute only.
A program may use at most 128 MiB of HBM per device.

v0:
```python
import jax
import jax.numpy as jnp
from jax import lax
from jax.sharding import PartitionSpec as P

HEADS = 8
WH = 8
WW = 16
SH = 4
SW = 8
EPSILON = 1e-05
MASKED = -1e30


def padded(shard, sides, width):
    for axis, dim in sides:
        size, length = (lax.axis_size(axis), shard.shape[dim])
        up = [(i, (i + 1) % size) for i in range(size - 1)]
        down = [(j, i) for i, j in up]
        last = lax.slice_in_dim(shard, length - width, length, axis=dim)
        first = lax.slice_in_dim(shard, 0, width, axis=dim)
        before = lax.ppermute(last, axis, up)
        after = lax.ppermute(first, axis, down)
        shard = jnp.concatenate([before, shard, after], axis=dim)
    return shard


def normalize(update):
    average = jnp.mean(update, axis=-1, keepdims=True)
    centered = update - average
    spread = jnp.mean(centered * centered, axis=-1, keepdims=True)
    inverse = lax.rsqrt(spread + EPSILON)
    return (centered * inverse, inverse)


def window_pattern(lon_count):
    query_index = jnp.arange(WH * lon_count, dtype=jnp.int32)
    key_index = jnp.arange(2 * WH * lon_count, dtype=jnp.int32)
    query_row = query_index // lon_count
    query_col = query_index % lon_count
    key_row = key_index // lon_count
    key_col = key_index % lon_count
    lat_same = ((query_row + SH) // WH)[:, None] == (key_row // WH)[None, :]
    lon_same = ((query_col + SW) // WW)[:, None] == ((key_col + SW) // WW)[None, :]
    self_key = ((query_row + SH)[:, None] == key_row[None, :]) & (
        query_col[:, None] == key_col[None, :]
    )
    return (lat_same & lon_same, self_key)


def attend(queries, keyvals, usable):
    row_count, lon_count, feature = queries.shape
    blocks = row_count // WH
    head_dim = feature // HEADS
    query_blocks = queries.reshape(blocks, WH * lon_count, HEADS, head_dim)
    kv_blocks = keyvals.reshape(blocks + 1, WH * lon_count, 2, HEADS, head_dim)
    key_pairs = jnp.concatenate([kv_blocks[:-1], kv_blocks[1:]], axis=1)
    use_blocks = usable.reshape(blocks + 1, WH * lon_count)
    use_pairs = jnp.concatenate([use_blocks[:-1], use_blocks[1:]], axis=1)
    inside, self_key = window_pattern(lon_count)
    allowed = inside[None] & (use_pairs[:, None, :] | self_key[None])
    scores = jnp.einsum(
        "nqhd,nkhd->nhqk", query_blocks, key_pairs[:, :, 0], preferred_element_type=jnp.float32
    ) * head_dim ** (-0.5)
    scores = jnp.where(allowed[:, None], scores, MASKED)
    highest = jnp.max(scores, axis=-1, keepdims=True)
    weights = jnp.exp(scores - highest)
    attn_prob = (weights / jnp.sum(weights, axis=-1, keepdims=True)).astype(jnp.bfloat16)
    mixture = jnp.einsum(
        "nhqk,nkhd->nqhd", attn_prob, key_pairs[:, :, 1], preferred_element_type=jnp.float32
    )
    return mixture.reshape(row_count, lon_count, feature).astype(jnp.bfloat16)


def guarded(active, function, operands):

    def skipped(values):
        return jax.tree.map(jnp.zeros_like, function(values))

    return lax.cond(active, function, skipped, operands)


def project(joined, merge_full, qkv_full, gain_full):
    update = jnp.einsum("rwj,jd->rwd", joined, merge_full, preferred_element_type=jnp.float32)
    normed, inverse = normalize(update)
    hidden = (normed * gain_full.astype(jnp.float32)).astype(jnp.bfloat16)
    projected = jnp.einsum("rwd,de->rwe", hidden, qkv_full, preferred_element_type=jnp.float32)
    feature = update.shape[-1]
    queries = projected[..., :feature].astype(jnp.bfloat16)
    keyvals = projected[..., feature:].astype(jnp.bfloat16)
    return (update, normed, inverse, hidden, queries, keyvals)


def section_forward(active, joined, usable, merge_full, qkv_full, gain_full, out_full):
    update, normed, inverse, hidden, queries, own_keys = guarded(
        active, lambda rows_own: project(rows_own, merge_full, qkv_full, gain_full), joined
    )
    keyvals = padded(own_keys, (("band", 0),), SH)

    def finish(operands):
        update_in, query_in, keyval_in, usable_in = operands
        mixture = attend(query_in, keyval_in, usable_in)
        result = (
            update_in
            + jnp.einsum("rwd,de->rwe", mixture, out_full, preferred_element_type=jnp.float32)
        ).astype(jnp.bfloat16)
        return (mixture, result)

    mixture, result = guarded(active, finish, (update, queries, keyvals, usable))
    return (result, (joined, normed, inverse, hidden, queries, keyvals, mixture))


def attend_back(out_full, operands):
    grad_out, queries, keyvals, mixture, usable = operands
    grad_mixture = jnp.einsum(
        "rwe,de->rwd", grad_out, out_full, preferred_element_type=jnp.float32
    ).astype(jnp.bfloat16)
    unused, pull_back = jax.vjp(
        lambda query_in, keyval_in: attend(query_in, keyval_in, usable), queries, keyvals
    )
    grad_query, grad_keyval = pull_back(grad_mixture)
    grad_outw = jnp.einsum("rwd,rwe->de", mixture, grad_out, preferred_element_type=jnp.float32)
    return (grad_query, grad_keyval, grad_outw)


def fold_rims(grad_keyval, row_count):
    rim_rows = jnp.concatenate([grad_keyval[:SH], grad_keyval[SH + row_count :]], axis=0)
    returned = padded(rim_rows, (("band", 0),), SH)
    own_part = grad_keyval[SH : SH + row_count].astype(jnp.float32)
    return jnp.concatenate(
        [
            own_part[:SH] + returned[:SH].astype(jnp.float32),
            own_part[SH : row_count - SH],
            own_part[row_count - SH :] + returned[3 * SH :].astype(jnp.float32),
        ],
        axis=0,
    ).astype(jnp.bfloat16)


def back_core(qkv_full, gain_full, grad_query, grad_keyown, grad_out, normed, inverse):
    grad_proj = jnp.concatenate([grad_query, grad_keyown], axis=-1)
    grad_hidden = jnp.einsum("rwe,de->rwd", grad_proj, qkv_full, preferred_element_type=jnp.float32)
    grad_normed = grad_hidden * gain_full.astype(jnp.float32)
    grad_update = (
        grad_out.astype(jnp.float32)
        + inverse
        * (
            grad_normed
            - jnp.mean(grad_normed, axis=-1, keepdims=True)
            - normed * jnp.mean(grad_normed * normed, axis=-1, keepdims=True)
        )
    ).astype(jnp.bfloat16)
    return (grad_proj, grad_hidden, grad_update)


def body(fields, cell_mask, merge_weight, qkv_weight, out_weight, norm_gain, out_cotangent):
    merge_rows, qkv_rows, out_rows, gain_rows = (
        lax.all_gather(merge_weight, "dp", axis=1, tiled=True),
        lax.all_gather(qkv_weight, "dp", axis=1, tiled=True),
        lax.all_gather(out_weight, "dp", axis=1, tiled=True),
        lax.all_gather(norm_gain, "dp", axis=1, tiled=True),
    )
    merge_full = merge_rows[0]
    qkv_full = qkv_rows[0]
    inputs = fields[0]
    cotangent = out_cotangent[0]
    micro_count, row_count, lon_count, feature = inputs.shape
    mask_ext = padded(cell_mask[0], (("band", 1),), SH)
    usable_ext = mask_ext == 1
    section_count = lax.axis_size("segment")
    half_count = section_count // 2
    section_rank = lax.axis_index("segment")
    merge_all, qkv_all, out_all, gain_all = (
        lax.all_gather(merge_rows, "segment", axis=0, tiled=True),
        lax.all_gather(qkv_rows, "segment", axis=0, tiled=True),
        lax.all_gather(out_rows, "segment", axis=0, tiled=True),
        lax.all_gather(gain_rows, "segment", axis=0, tiled=True),
    )
    local_count = micro_count // section_count
    always = jnp.array(True)
    shipped = [[] for index in range(section_count)]
    pick = section_rank * local_count + 0
    inputs_now = lax.dynamic_index_in_dim(inputs, pick, 0, keepdims=False)
    cotangent_now = lax.dynamic_index_in_dim(cotangent, pick, 0, keepdims=False)
    usable_now = lax.dynamic_index_in_dim(usable_ext, pick, 0, keepdims=False)
    outputs = []
    records = []
    for index in range(section_count):
        chain_in = inputs_now if index == 0 else outputs[index - 1]
        side_in = inputs_now if index < half_count else outputs[section_count - 1 - index]
        joined = jnp.concatenate([chain_in, side_in], axis=-1)
        result, record = section_forward(
            always,
            joined,
            usable_now,
            merge_all[index],
            qkv_all[index],
            gain_all[index],
            out_all[index],
        )
        outputs.append(result)
        records.append(record)
    flows = [None] * section_count
    for index in range(section_count - 1, -1, -1):
        grad_out = (
            cotangent_now if index == section_count - 1 else flows[index].astype(jnp.bfloat16)
        )
        joined, normed, inverse, hidden, queries, keyvals, mixture = records[index]
        grad_query, grad_keyval, unused = attend_back(
            out_all[index], (grad_out, queries, keyvals, mixture, usable_now)
        )
        grad_keyown = fold_rims(grad_keyval, row_count)
        grad_proj, unused, grad_update = back_core(
            qkv_all[index], gain_all[index], grad_query, grad_keyown, grad_out, normed, inverse
        )
        grad_joined = jnp.einsum(
            "rwd,jd->rwj", grad_update, merge_all[index], preferred_element_type=jnp.float32
        )
        grad_chain = grad_joined[..., :feature].astype(jnp.bfloat16).astype(jnp.float32)
        grad_side = grad_joined[..., feature:].astype(jnp.bfloat16).astype(jnp.float32)
        if index > 0:
            flows[index - 1] = grad_chain
        if index >= half_count:
            target = section_count - 1 - index
            flows[target] = flows[target] + grad_side
        shipped[index].append(
            (outputs[index], joined, grad_update, hidden, grad_proj, mixture, grad_out)
        )
    packed = tuple(
        (
            jnp.stack([jnp.stack([shipped[index][0][field]]) for index in range(section_count)])
            for field in range(7)
        )
    )
    home = (
        lax.all_to_all(packed[0], "segment", split_axis=0, concat_axis=1, tiled=True),
        lax.all_to_all(packed[1], "segment", split_axis=0, concat_axis=1, tiled=True),
        lax.all_to_all(packed[2], "segment", split_axis=0, concat_axis=1, tiled=True),
        lax.all_to_all(packed[3], "segment", split_axis=0, concat_axis=1, tiled=True),
        lax.all_to_all(packed[4], "segment", split_axis=0, concat_axis=1, tiled=True),
        lax.all_to_all(packed[5], "segment", split_axis=0, concat_axis=1, tiled=True),
        lax.all_to_all(packed[6], "segment", split_axis=0, concat_axis=1, tiled=True),
    )
    joined_all, grad_update_all, hidden_all, grad_proj_all, mixture_all, grad_out_all = [
        part[0] for part in home[1:]
    ]
    grad_merge = jnp.einsum(
        "mrwj,mrwd->jd", joined_all, grad_update_all, preferred_element_type=jnp.float32
    )
    grad_qkv = jnp.einsum(
        "mrwd,mrwe->de", hidden_all, grad_proj_all, preferred_element_type=jnp.float32
    )
    grad_outw = jnp.einsum(
        "mrwd,mrwe->de", mixture_all, grad_out_all, preferred_element_type=jnp.float32
    )
    update_all = jnp.einsum(
        "mrwj,jd->mrwd", joined_all, merge_full, preferred_element_type=jnp.float32
    )
    normed_all, unused = normalize(update_all)
    grad_hidden_all = jnp.einsum(
        "mrwe,de->mrwd", grad_proj_all, qkv_full, preferred_element_type=jnp.float32
    )
    grad_gain = jnp.sum(grad_hidden_all * normed_all, axis=(0, 1, 2))
    grad_sums = (grad_merge, grad_qkv, grad_outw, grad_gain)
    section_home = home[0][None]
    merge_part_sum, qkv_part_sum, out_part_sum, gain_part_sum = (
        lax.psum_scatter(
            grad_sums[0][None].astype(jnp.bfloat16), "dp", scatter_dimension=1, tiled=True
        ).astype(jnp.float32),
        lax.psum_scatter(
            grad_sums[1][None].astype(jnp.bfloat16), "dp", scatter_dimension=1, tiled=True
        ).astype(jnp.float32),
        lax.psum_scatter(
            grad_sums[2][None].astype(jnp.bfloat16), "dp", scatter_dimension=1, tiled=True
        ).astype(jnp.float32),
        lax.psum_scatter(
            grad_sums[3][None].astype(jnp.bfloat16), "dp", scatter_dimension=1, tiled=True
        ).astype(jnp.float32),
    )
    merge_grad, qkv_grad, out_grad, gain_grad = (
        lax.psum(merge_part_sum.astype(jnp.bfloat16), "band").astype(jnp.float32),
        lax.psum(qkv_part_sum.astype(jnp.bfloat16), "band").astype(jnp.float32),
        lax.psum(out_part_sum.astype(jnp.bfloat16), "band").astype(jnp.float32),
        lax.psum(gain_part_sum.astype(jnp.bfloat16), "band").astype(jnp.float32),
    )
    return (section_home, merge_grad, qkv_grad, out_grad, gain_grad)


def solution(mesh):
    return jax.shard_map(
        body,
        mesh=mesh,
        in_specs=(
            P("dp", None, "band", None, None),
            P("dp", None, "band", None),
            P("segment", "dp", None),
            P("segment", "dp", None),
            P("segment", "dp", None),
            P("segment", "dp"),
            P("dp", None, "band", None, None),
        ),
        out_specs=(
            P("segment", "dp", None, "band", None, None),
            P("segment", "dp", None),
            P("segment", "dp", None),
            P("segment", "dp", None),
            P("segment", "dp"),
        ),
        check_vma=False,
    )
```

profile of v0, /device:TPU:0, one launch (start us, length us, event | category | flops | bytes accessed | tf_op | source)
XLA Modules:
  0.0 377.2 jit_solution(2174182986141230632)
XLA Ops:
  8.8 30.4 %all-gather.7.cloned.1.call-done = bf16[1,1024,512]{2,1,0:T(8,128)(2,1)} async-done(((bf16[1,256,512]{2,1,0:T(8,128)(2,1)}), bf16[1,1024,512]{2,1,0:T(8,128)(2,1)}) %all-gather.7.cloned.1.call-update) | async-done | bytes 1048592 | tf_op jit(solution)/shard_map/all_gather | solution.py:158
  39.2 32.6 %all-gather.11.cloned.1.call-done = bf16[1,512,1536]{2,1,0:T(8,128)(2,1)} async-done(((bf16[1,128,1536]{2,1,0:T(8,128)(2,1)}), bf16[1,512,1536]{2,1,0:T(8,128)(2,1)}) %all-gather.11.cloned.1.call-update) | async-done | bytes 1572880 | tf_op jit(solution)/shard_map/all_gather | solution.py:159
  73.2 4.5 %collective-permute-start.2 = (s32[2,4,16]{2,1,0:T(4,128)S(1)}, s32[2,4,16]{2,1,0:T(4,128)S(1)}, u32[]{:S(2)}, u32[]{:S(2)}) collective-permute-start(s32[2,4,16]{2,1,0:T(4,128)S(1)} %get-tuple-element.47), channel_id=1, source_target_pairs={{0,1},{1,2},{2,3},{4,5},{5,6},{6,7},{8,9},{9,10},{10,11},{12,13},{... | collective-permute-start | bytes 1544 | tf_op jit(solution)/shard_map/ppermute | solution.py:22
  77.8 10.6 %all_gather.30 = bf16[1,512,512]{2,1,0:T(8,128)(2,1)} all-gather(bf16[1,128,512]{2,1,0:T(8,128)(2,1)S(1)} %copy-done.33), channel_id=1, replica_groups=mesh['dp'=4,'segment'=2,'band'=4] {'dp'}, dimensions={1}, use_global_device_ids=true | all-gather | bytes 655360 | tf_op jit(solution)/shard_map/all_gather | solution.py:160
  88.5 7.1 %all_gather.26 = bf16[1,512]{1,0:T(2,128)(2,1)S(1)} all-gather(bf16[1,128]{1,0:T(2,128)(2,1)S(1)} %copy-done.44), channel_id=1, replica_groups=mesh['dp'=4,'segment'=2,'band'=4] {'dp'}, dimensions={1}, use_global_device_ids=true | all-gather | bytes 1280 | tf_op jit(solution)/shard_map/all_gather | solution.py:161
  102.3 3.4 collective-permute-start
  125.8 3.4 collective-permute-start.4
  132.7 3.8 %collective-permute-done.5 = bf16[4,16,1024]{2,1,0:T(8,128)(2,1)S(1)} collective-permute-done((bf16[4,16,1024]{2,1,0:T(8,128)(2,1)S(1)}, bf16[4,16,1024]{2,1,0:T(8,128)(2,1)S(1)}, u32[]{:S(2)}, u32[]{:S(2)}) %collective-permute-start.5) | collective-permute-done | bytes 131104 | tf_op jit(solution)/shard_map/ppermute | solution.py:23
  149.3 4.1 %all-to-all-start.5 = ((bf16[2,1,8,16,512]{4,3,2,1,0:T(8,128)(2,1)}), bf16[2,1,8,16,512]{4,3,2,1,0:T(8,128)(2,1)}, u32[]{:S(2)}, u32[]{:S(2)}) async-start(bf16[2,1,8,16,512]{4,3,2,1,0:T(8,128)(2,1)} %pad_maximum_fusion.13), calls=%async_computation.7 | async-start | bytes 524288 | tf_op jit(solution)/shard_map/all_to_all | solution.py:241
  161.1 3.4 collective-permute-start.6
  167.8 4.1 %collective-permute-done.7 = bf16[4,16,1024]{2,1,0:T(8,128)(2,1)S(1)} collective-permute-done((bf16[4,16,1024]{2,1,0:T(8,128)(2,1)S(1)}, bf16[4,16,1024]{2,1,0:T(8,128)(2,1)S(1)}, u32[]{:S(2)}, u32[]{:S(2)}) %collective-permute-start.7) | collective-permute-done | bytes 131104 | tf_op jit(solution)/shard_map/ppermute | solution.py:23
  183.2 3.4 collective-permute-start.8
  189.1 4.4 %collective-permute-done.9 = bf16[4,16,1024]{2,1,0:T(8,128)(2,1)S(1)} collective-permute-done((bf16[4,16,1024]{2,1,0:T(8,128)(2,1)S(1)}, bf16[4,16,1024]{2,1,0:T(8,128)(2,1)S(1)}, u32[]{:S(2)}, u32[]{:S(2)}) %collective-permute-start.9) | collective-permute-done | bytes 131104 | tf_op jit(solution)/shard_map/ppermute | solution.py:23
  196.0 3.9 %all_to_all.28 = bf16[2,1,8,16,512]{4,3,2,1,0:T(8,128)(2,1)S(1)} all-to-all(bf16[2,1,8,16,512]{4,3,2,1,0:T(8,128)(2,1)S(1)} %pad_maximum_fusion.14), channel_id=1, replica_groups=mesh['dp'=4,'segment'=2,'band'=4] {'segment'}, dimensions={0} | all-to-all | bytes 524288 | tf_op jit(solution)/shard_map/all_to_all | solution.py:242
  203.0 3.5 all-to-all-start.1
  208.2 3.9 %all_to_all.29 = bf16[2,1,8,16,512]{4,3,2,1,0:T(8,128)(2,1)S(1)} all-to-all(bf16[2,1,8,16,512]{4,3,2,1,0:T(8,128)(2,1)S(1)} %pad_maximum_fusion.11), channel_id=1, replica_groups=mesh['dp'=4,'segment'=2,'band'=4] {'segment'}, dimensions={0} | all-to-all | bytes 524288 | tf_op jit(solution)/shard_map/all_to_all | solution.py:238
  214.4 3.4 all-to-all-start.3
  220.1 4.4 %all_to_all.30 = bf16[2,1,8,16,1536]{4,3,2,1,0:T(8,128)(2,1)S(1)} all-to-all(bf16[2,1,8,16,1536]{4,3,2,1,0:T(8,128)(2,1)S(1)} %pad_maximum_fusion), channel_id=1, replica_groups=mesh['dp'=4,'segment'=2,'band'=4] {'segment'}, dimensions={0} | all-to-all | bytes 1572864 | tf_op jit(solution)/shard_map/all_to_all | solution.py:240
  230.3 26.1 %reduce-scatter.7.cloned.1.call-done = bf16[1,256,512]{2,1,0:T(8,128)(2,1)} async-done(((bf16[1,1024,512]{2,1,0:T(8,128)(2,1)}), bf16[1,256,512]{2,1,0:T(8,128)(2,1)}) %reduce-scatter.7.cloned.1.call-update) | async-done | bytes 262160 | tf_op jit(solution)/shard_map/reduce_scatter | solution.py:267
  256.3 34.2 %reduce-scatter.9.cloned.1.call-done = bf16[1,128,1536]{2,1,0:T(8,128)(2,1)} async-done(((bf16[1,512,1536]{2,1,0:T(8,128)(2,1)}), bf16[1,128,1536]{2,1,0:T(8,128)(2,1)}) %reduce-scatter.9.cloned.1.call-update) | async-done | bytes 393232 | tf_op jit(solution)/shard_map/reduce_scatter | solution.py:270
  291.0 3.9 %all_to_all.31 = bf16[2,1,8,16,512]{4,3,2,1,0:T(8,128)(2,1)S(1)} all-to-all(bf16[2,1,8,16,512]{4,3,2,1,0:T(8,128)(2,1)S(1)} %pad_maximum_fusion.10), channel_id=1, replica_groups=mesh['dp'=4,'segment'=2,'band'=4] {'segment'}, dimensions={0} | all-to-all | bytes 524288 | tf_op jit(solution)/shard_map/all_to_all | solution.py:236
  295.0 23.0 %reduce-scatter.13.cloned.1.call-done = bf16[128,1]{1,0:T(8,128)(2,1)} async-done(((bf16[512,1]{1,0:T(8,128)(2,1)}), bf16[128,1]{1,0:T(8,128)(2,1)}) %reduce-scatter.13.cloned.1.call-update) | async-done | bytes 272
  318.8 11.7 %psum.31 = bf16[1,128]{1,0:T(2,128)(2,1)S(1)} all-reduce(bf16[1,128]{1,0:T(2,128)(2,1)S(1)} %copy.77), channel_id=1, replica_groups=mesh['dp'=4,'segment'=2,'band'=4] {'band'}, use_global_device_ids=true, to_apply=%region_28.29 | all-reduce | flops 128 | bytes 512 | tf_op jit(solution)/shard_map/psum | solution.py:284
  331.0 33.2 %all-reduce.11.cloned.1.call-done = (bf16[1,256,512]{2,1,0:T(8,128)(2,1)}, bf16[1,128,1536]{2,1,0:T(8,128)(2,1)}, bf16[1,128,512]{2,1,0:T(8,128)(2,1)}) async-done(((bf16[1,256,512]{2,1,0:T(8,128)(2,1)}, bf16[1,128,1536]{2,1,0:T(8,128)(2,1)}, bf16[1,128,512]{2,1,0:T(8,128)(2,1)}), (bf16[1,256,512]{2,1,0:T(8,128)(2,1)}, bf16[1,128,1536]{2,1,0:T(8,128)(2,1)}, ...) | async-done | bytes 786448 | tf_op jit(solution)/shard_map/psum | solution.py:281
  (268 shorter events, 95.1 us)
Async XLA Ops:
  7.2 90.8 %copy-start = (bf16[1,2,8,16,512]{4,3,2,1,0:T(8,128)(2,1)S(1)}, bf16[1,2,8,16,512]{4,3,2,1,0:T(8,128)(2,1)}, u32[]{:S(2)}) copy-start(bf16[1,2,8,16,512]{4,3,2,1,0:T(8,128)(2,1)} %param.7) | copy-start | bytes 786436
  7.2 31.9 %all-gather.7.cloned.1.call-start = ((), (), s32[]{:S(2)}) async-start(), calls=%async_computation.11 | async-start | bytes 1310720 | tf_op jit(solution)/shard_map/all_gather | solution.py:158
  7.9 63.9 %all-gather.11.cloned.1.call-start = ((), (), s32[]{:S(2)}) async-start(), calls=%async_computation.13 | async-start | bytes 1966080 | tf_op jit(solution)/shard_map/all_gather | solution.py:159
  8.7 89.8 %all-gather.9.cloned.1.call-start = ((), (), s32[]{:S(2)}) async-start(), calls=%async_computation.12 | async-start | bytes 3145728 | tf_op jit(solution)/shard_map/all_gather | solution.py:174
  39.1 61.2 %all-gather.13.cloned.1.call-start = ((), (), s32[]{:S(2)}) async-start(), calls=%async_computation.14 | async-start | bytes 4718592 | tf_op jit(solution)/shard_map/all_gather | solution.py:175
  71.8 38.5 %all-gather.15.cloned.1.call-start = ((), (), s32[]{:S(2)}) async-start(), calls=%async_computation.15 | async-start | bytes 1572864 | tf_op jit(solution)/shard_map/all_gather | solution.py:176
  71.9 26.2 %collective-permute-start.3 = (s32[2,4,16]{2,1,0:T(4,128)S(1)}, s32[2,4,16]{2,1,0:T(4,128)S(1)}, u32[]{:S(2)}, u32[]{:S(2)}) collective-permute-start(s32[2,4,16]{2,1,0:T(4,128)S(1)} %get-tuple-element.46), channel_id=1, source_target_pairs={{1,0},{2,1},{3,2},{5,4},{6,5},{7,6},{9,8},{10,9},{11,10},{13,12},{... | collective-permute-start | bytes 1544 | tf_op jit(solution)/shard_map/ppermute | solution.py:23
  73.2 24.9 %collective-permute-start.2 = (s32[2,4,16]{2,1,0:T(4,128)S(1)}, s32[2,4,16]{2,1,0:T(4,128)S(1)}, u32[]{:S(2)}, u32[]{:S(2)}) collective-permute-start(s32[2,4,16]{2,1,0:T(4,128)S(1)} %get-tuple-element.47), channel_id=1, source_target_pairs={{0,1},{1,2},{2,3},{4,5},{5,6},{6,7},{8,9},{9,10},{10,11},{12,13},{... | collective-permute-start | bytes 1544 | tf_op jit(solution)/shard_map/ppermute | solution.py:22
  102.3 10.2 %collective-permute-start = (bf16[4,16,1024]{2,1,0:T(8,128)(2,1)S(1)}, bf16[4,16,1024]{2,1,0:T(8,128)(2,1)S(1)}, u32[]{:S(2)}, u32[]{:S(2)}) collective-permute-start(bf16[4,16,1024]{2,1,0:T(8,128)(2,1)S(1)} %get-tuple-element.35), channel_id=1, source_target_pairs={{0,1},{1,2},{2,3},{4,5},{5,6},{6,7},{8,9},{9,10},{10,11},{12,13},{... | collective-permute-start | bytes 393224 | tf_op jit(solution)/shard_map/ppermute | solution.py:22
  105.7 7.2 %collective-permute-start.1 = (bf16[4,16,1024]{2,1,0:T(8,128)(2,1)S(1)}, bf16[4,16,1024]{2,1,0:T(8,128)(2,1)S(1)}, u32[]{:S(2)}, u32[]{:S(2)}) collective-permute-start(bf16[4,16,1024]{2,1,0:T(8,128)(2,1)S(1)} %get-tuple-element.36), channel_id=1, source_target_pairs={{1,0},{2,1},{3,2},{5,4},{6,5},{7,6},{9,8},{10,9},{11,10},{13,12},{... | collective-permute-start | bytes 393224 | tf_op jit(solution)/shard_map/ppermute | solution.py:23
  125.8 6.9 %collective-permute-start.4 = (bf16[4,16,1024]{2,1,0:T(8,128)(2,1)}, bf16[4,16,1024]{2,1,0:T(8,128)(2,1)S(1)}, u32[]{:S(2)}, u32[]{:S(2)}) collective-permute-start(bf16[4,16,1024]{2,1,0:T(8,128)(2,1)} %get-tuple-element.33), channel_id=1, source_target_pairs={{0,1},{1,2},{2,3},{4,5},{5,6},{6,7},{8,9},{9,10},{10,11},{12,13},{... | collective-permute-start | bytes 393224 | tf_op jit(solution)/shard_map/ppermute | solution.py:22
  129.2 7.3 %collective-permute-start.5 = (bf16[4,16,1024]{2,1,0:T(8,128)(2,1)S(1)}, bf16[4,16,1024]{2,1,0:T(8,128)(2,1)S(1)}, u32[]{:S(2)}, u32[]{:S(2)}) collective-permute-start(bf16[4,16,1024]{2,1,0:T(8,128)(2,1)S(1)} %get-tuple-element.34), channel_id=1, source_target_pairs={{1,0},{2,1},{3,2},{5,4},{6,5},{7,6},{9,8},{10,9},{11,10},{13,12},{... | collective-permute-start | bytes 393224 | tf_op jit(solution)/shard_map/ppermute | solution.py:23
  149.3 46.7 %all-to-all-start.5 = ((bf16[2,1,8,16,512]{4,3,2,1,0:T(8,128)(2,1)}), bf16[2,1,8,16,512]{4,3,2,1,0:T(8,128)(2,1)}, u32[]{:S(2)}, u32[]{:S(2)}) async-start(bf16[2,1,8,16,512]{4,3,2,1,0:T(8,128)(2,1)} %pad_maximum_fusion.13), calls=%async_computation.7 | async-start | bytes 524288 | tf_op jit(solution)/shard_map/all_to_all | solution.py:241
  153.4 76.8 %reduce-scatter.11.cloned.1.call-start = ((), (), s32[]{:S(2)}) async-start(), calls=%async_computation.18 | async-start | bytes 655360 | tf_op jit(solution)/shard_map/reduce_scatter | solution.py:273
  161.1 6.7 %collective-permute-start.6 = (bf16[4,16,1024]{2,1,0:T(8,128)(2,1)S(1)}, bf16[4,16,1024]{2,1,0:T(8,128)(2,1)S(1)}, u32[]{:S(2)}, u32[]{:S(2)}) collective-permute-start(bf16[4,16,1024]{2,1,0:T(8,128)(2,1)S(1)} %get-tuple-element.29), channel_id=1, source_target_pairs={{0,1},{1,2},{2,3},{4,5},{5,6},{6,7},{8,9},{9,10},{10,11},{12,13},{... | collective-permute-start | bytes 393224 | tf_op jit(solution)/shard_map/ppermute | solution.py:22
  164.4 7.5 %collective-permute-start.7 = (bf16[4,16,1024]{2,1,0:T(8,128)(2,1)S(1)}, bf16[4,16,1024]{2,1,0:T(8,128)(2,1)S(1)}, u32[]{:S(2)}, u32[]{:S(2)}) collective-permute-start(bf16[4,16,1024]{2,1,0:T(8,128)(2,1)S(1)} %get-tuple-element.30), channel_id=1, source_target_pairs={{1,0},{2,1},{3,2},{5,4},{6,5},{7,6},{9,8},{10,9},{11,10},{13,12},{... | collective-permute-start | bytes 393224 | tf_op jit(solution)/shard_map/ppermute | solution.py:23
  183.2 5.9 %collective-permute-start.8 = (bf16[4,16,1024]{2,1,0:T(8,128)(2,1)S(1)}, bf16[4,16,1024]{2,1,0:T(8,128)(2,1)S(1)}, u32[]{:S(2)}, u32[]{:S(2)}) collective-permute-start(bf16[4,16,1024]{2,1,0:T(8,128)(2,1)S(1)} %get-tuple-element.23), channel_id=1, source_target_pairs={{0,1},{1,2},{2,3},{4,5},{5,6},{6,7},{8,9},{9,10},{10,11},{12,13},{... | collective-permute-start | bytes 393224 | tf_op jit(solution)/shard_map/ppermute | solution.py:22
  186.6 6.9 %collective-permute-start.9 = (bf16[4,16,1024]{2,1,0:T(8,128)(2,1)S(1)}, bf16[4,16,1024]{2,1,0:T(8,128)(2,1)S(1)}, u32[]{:S(2)}, u32[]{:S(2)}) collective-permute-start(bf16[4,16,1024]{2,1,0:T(8,128)(2,1)S(1)} %get-tuple-element.24), channel_id=1, source_target_pairs={{1,0},{2,1},{3,2},{5,4},{6,5},{7,6},{9,8},{10,9},{11,10},{13,12},{... | collective-permute-start | bytes 393224 | tf_op jit(solution)/shard_map/ppermute | solution.py:23
  203.0 5.2 %all-to-all-start.1 = ((bf16[2,1,8,16,1024]{4,3,2,1,0:T(8,128)(2,1)}), bf16[2,1,8,16,1024]{4,3,2,1,0:T(8,128)(2,1)S(1)}, u32[]{:S(2)}, u32[]{:S(2)}) async-start(bf16[2,1,8,16,1024]{4,3,2,1,0:T(8,128)(2,1)} %pad_maximum_fusion.1), calls=%async_computation.1 | async-start | bytes 1048576 | tf_op jit(solution)/shard_map/all_to_all | solution.py:237
  206.5 49.9 %reduce-scatter.7.cloned.1.call-start = ((), (), s32[]{:S(2)}) async-start(), calls=%async_computation.16 | async-start | bytes 1310720 | tf_op jit(solution)/shard_map/reduce_scatter | solution.py:267
  214.4 5.0 %all-to-all-start.3 = ((bf16[2,1,8,16,512]{4,3,2,1,0:T(8,128)(2,1)}), bf16[2,1,8,16,512]{4,3,2,1,0:T(8,128)(2,1)S(1)}, u32[]{:S(2)}, u32[]{:S(2)}) async-start(bf16[2,1,8,16,512]{4,3,2,1,0:T(8,128)(2,1)} %pad_maximum_fusion.12), calls=%async_computation.4 | async-start | bytes 524288 | tf_op jit(solution)/shard_map/all_to_all | solution.py:239
  217.8 72.7 %reduce-scatter.9.cloned.1.call-start = ((), (), s32[]{:S(2)}) async-start(), calls=%async_computation.17 | async-start | bytes 1966080 | tf_op jit(solution)/shard_map/reduce_scatter | solution.py:270
  227.3 90.7 %reduce-scatter.13.cloned.1.call-start = ((), (), s32[]{:S(2)}) async-start(), calls=%async_computation.19 | async-start | bytes 163840
  230.2 134.1 %all-reduce.11.cloned.1.call-start = ((), (), s32[]{:S(2)}) async-start(), calls=%async_computation.20 | async-start | bytes 1572864 | tf_op jit(solution)/shard_map/psum | solution.py:281
  (46 other events, 627.2 us)
Sparse Core Ops, SparseCore 0:
  9.9 29.2 all-gather.6
  40.9 30.8 all-gather.10
  73.4 10.5 all-gather.8
  85.4 13.2 all-gather.12
  100.1 10.1 all-gather.14
  202.2 23.2 reduce-scatter.10
  228.3 27.9 reduce-scatter.6
  259.3 31.1 reduce-scatter.8
  293.8 24.1 reduce-scatter.12
  320.4 43.7 all-reduce.10
where the time goes:
time: 379 us; the launch traced here: 377 us
  waiting for transfers between devices  203 us (54%)
  blocking collectives  47.4 us (13%)
  starting transfers between devices  36.4 us (10%)
  matrix products  32 us (8%)
  local copies, waits for them, and re-layouts  23.7 us (6%)
  other arithmetic  18.8 us (5%)
  between operations  15.6 us (4%)
    reduce_scatter x1, waiting for transfers between devices, body(): lax.psum_scatter(grad_sums[1][None].astype(jnp.bfloat16), 'dp', scatter_d...  34.2 us
    psum x1, waiting for transfers between devices, body(): lax.psum(merge_part_sum.astype(jnp.bfloat16), 'band').astype(jnp.float32)  33.2 us
    all_gather x1, waiting for transfers between devices, body(): lax.all_gather(qkv_weight, 'dp', axis=1, tiled=True)  32.6 us
    all_gather x1, waiting for transfers between devices, body(): lax.all_gather(merge_weight, 'dp', axis=1, tiled=True)  30.4 us
    reduce_scatter x1, waiting for transfers between devices, body(): lax.psum_scatter(grad_sums[0][None].astype(jnp.bfloat16), 'dp', scatter_d...  26.1 us
    unnamed x11, waiting for transfers between devices  24.5 us
    ppermute x5, starting transfers between devices, padded(): before = lax.ppermute(last, axis, up)  18.1 us
    ppermute x5, waiting for transfers between devices, padded(): after = lax.ppermute(first, axis, down)  12.6 us
  transfers between devices with their start and end apart: 23, of which 16 were waited for; matrix products, arithmetic and copies ran while one was open for 10% of the time, Pallas kernels for 0%

commit v1 on v0

--- a/solution.py
+++ b/solution.py
@@ -10,6 +10,12 @@
 SW = 8
 EPSILON = 1e-05
 MASKED = -1e30
+
+
+def summed_here(x, name):
+    parts = lax.all_gather(x, name, axis=0, tiled=False)
+    total = parts.sum(axis=0)
+    return total
 
 
 def padded(shard, sides, width):
@@ -278,7 +284,7 @@
         ).astype(jnp.float32),
     )
     merge_grad, qkv_grad, out_grad, gain_grad = (
-        lax.psum(merge_part_sum.astype(jnp.bfloat16), "band").astype(jnp.float32),
+        summed_here(merge_part_sum.astype(jnp.bfloat16), "band").astype(jnp.float32),
         lax.psum(qkv_part_sum.astype(jnp.bfloat16), "band").astype(jnp.float32),
         lax.psum(out_part_sum.astype(jnp.bfloat16), "band").astype(jnp.float32),
         lax.psum(gain_part_sum.astype(jnp.bfloat16), "band").astype(jnp.float32),

time: 379 us -> 398 us (1.050)
  waiting for transfers between devices: 203 us -> 224 us
    reduce_scatter x1, waiting for transfers between devices: 26.1 us -> 0.02 us  [body(): lax.psum_scatter(grad_sums[0][None].astype(jnp.bfloat16), 'dp', scatter_d...]
    reduce_scatter x1, waiting for transfers between devices: 0.02 us -> 25.7 us  [body(): lax.psum_scatter(grad_sums[2][None].astype(jnp.bfloat16), 'dp', scatter_d...]
    all_gather x0 -> x1, waiting for transfers between devices: none -> 16.3 us  [summed_here(): parts = lax.all_gather(x, name, axis=0, tiled=False)]
    psum x1, waiting for transfers between devices: 33.2 us -> 38.2 us  [body(): lax.psum(qkv_part_sum.astype(jnp.bfloat16), 'band').astype(jnp.float32)]
    unnamed x11 -> x12, waiting for transfers between devices: 24.5 us -> 25.1 us
  transfers between devices with their start and end apart: 23 -> 24, of which waited for: 16 -> 16; matrix products, arithmetic and copies ran while one was open for 10% -> 14% of each run, Pallas kernels for 0% -> 0%
where the time goes in v1:
time: 398 us; the launch traced here: 396 us
  waiting for transfers between devices  224 us (56%)
  blocking collectives  47.5 us (12%)
  starting transfers between devices  35.9 us (9%)
  matrix products  33.5 us (8%)
  local copies, waits for them, and re-layouts  21.3 us (5%)
  other arithmetic  18.9 us (5%)
  between operations  15.4 us (4%)
    psum x1, waiting for transfers between devices, body(): lax.psum(qkv_part_sum.astype(jnp.bfloat16), 'band').astype(jnp.float32)  38.2 us
    reduce_scatter x1, waiting for transfers between devices, body(): lax.psum_scatter(grad_sums[1][None].astype(jnp.bfloat16), 'dp', scatter_d...  34.1 us
    all_gather x1, waiting for transfers between devices, body(): lax.all_gather(qkv_weight, 'dp', axis=1, tiled=True)  32.6 us
    all_gather x1, waiting for transfers between devices, body(): lax.all_gather(merge_weight, 'dp', axis=1, tiled=True)  30.4 us
    reduce_scatter x1, waiting for transfers between devices, body(): lax.psum_scatter(grad_sums[2][None].astype(jnp.bfloat16), 'dp', scatter_d...  25.7 us
    unnamed x12, waiting for transfers between devices  25.1 us
    ppermute x5, starting transfers between devices, padded(): before = lax.ppermute(last, axis, up)  17.5 us
    all_gather x1, waiting for transfers between devices, summed_here(): parts = lax.all_gather(x, name, axis=0, tiled=False)  16.3 us
  transfers between devices with their start and end apart: 24, of which 16 were waited for; matrix products, arithmetic and copies ran while one was open for 14% of the time, Pallas kernels for 0%

profile of v1, /device:TPU:0, one launch (start us, length us, event | category | flops | bytes accessed | tf_op | source)
XLA Modules:
  0.0 396.5 jit_solution(17636620124839370776)
XLA Ops:
  8.8 30.4 %all-gather.9.cloned.1.call-done = bf16[1,1024,512]{2,1,0:T(8,128)(2,1)} async-done(((bf16[1,256,512]{2,1,0:T(8,128)(2,1)}), bf16[1,1024,512]{2,1,0:T(8,128)(2,1)}) %all-gather.9.cloned.1.call-update) | async-done | bytes 1048592 | tf_op jit(solution)/shard_map/all_gather | solution.py:164
  39.2 32.6 %all-gather.13.cloned.1.call-done = bf16[1,512,1536]{2,1,0:T(8,128)(2,1)} async-done(((bf16[1,128,1536]{2,1,0:T(8,128)(2,1)}), bf16[1,512,1536]{2,1,0:T(8,128)(2,1)}) %all-gather.13.cloned.1.call-update) | async-done | bytes 1572880 | tf_op jit(solution)/shard_map/all_gather | solution.py:165
  73.2 4.5 %collective-permute-start.2 = (s32[2,4,16]{2,1,0:T(4,128)S(1)}, s32[2,4,16]{2,1,0:T(4,128)S(1)}, u32[]{:S(2)}, u32[]{:S(2)}) collective-permute-start(s32[2,4,16]{2,1,0:T(4,128)S(1)} %get-tuple-element.46), channel_id=1, source_target_pairs={{0,1},{1,2},{2,3},{4,5},{5,6},{6,7},{8,9},{9,10},{10,11},{12,13},{... | collective-permute-start | bytes 1544 | tf_op jit(solution)/shard_map/ppermute | solution.py:28
  77.8 10.6 %all_gather.36 = bf16[1,512,512]{2,1,0:T(8,128)(2,1)} all-gather(bf16[1,128,512]{2,1,0:T(8,128)(2,1)S(1)} %copy-done.47), channel_id=1, replica_groups=mesh['dp'=4,'segment'=2,'band'=4] {'dp'}, dimensions={1}, use_global_device_ids=true | all-gather | bytes 655360 | tf_op jit(solution)/shard_map/all_gather | solution.py:166
  88.5 7.1 %all_gather.32 = bf16[1,512]{1,0:T(2,128)(2,1)S(1)} all-gather(bf16[1,128]{1,0:T(2,128)(2,1)S(1)} %copy-done.59), channel_id=1, replica_groups=mesh['dp'=4,'segment'=2,'band'=4] {'dp'}, dimensions={1}, use_global_device_ids=true | all-gather | bytes 1280 | tf_op jit(solution)/shard_map/all_gather | solution.py:167
  102.9 3.4 collective-permute-start
  123.0 4.2 %all-to-all-start.1 = ((bf16[2,1,8,16,1024]{4,3,2,1,0:T(8,128)(2,1)}), bf16[2,1,8,16,1024]{4,3,2,1,0:T(8,128)(2,1)}, u32[]{:S(2)}, u32[]{:S(2)}) async-start(bf16[2,1,8,16,1024]{4,3,2,1,0:T(8,128)(2,1)} %pad_maximum_fusion.1), calls=%async_computation.1 | async-start | bytes 1048576 | tf_op jit(solution)/shard_map/all_to_all | solution.py:243
  127.7 3.4 collective-permute-start.4
  134.8 3.8 collective-permute-done.5
  159.0 4.3 %collective-permute-done.7 = bf16[4,16,1024]{2,1,0:T(8,128)(2,1)S(1)} collective-permute-done((bf16[4,16,1024]{2,1,0:T(8,128)(2,1)S(1)}, bf16[4,16,1024]{2,1,0:T(8,128)(2,1)S(1)}, u32[]{:S(2)}, u32[]{:S(2)}) %collective-permute-start.7) | collective-permute-done | bytes 131104 | tf_op jit(solution)/shard_map/ppermute | solution.py:29
  179.8 3.4 collective-permute-start.8
  185.7 4.4 %collective-permute-done.9 = bf16[4,16,1024]{2,1,0:T(8,128)(2,1)S(1)} collective-permute-done((bf16[4,16,1024]{2,1,0:T(8,128)(2,1)S(1)}, bf16[4,16,1024]{2,1,0:T(8,128)(2,1)S(1)}, u32[]{:S(2)}, u32[]{:S(2)}) %collective-permute-start.9) | collective-permute-done | bytes 131104 | tf_op jit(solution)/shard_map/ppermute | solution.py:29
  192.7 3.9 all_to_all.28
  201.0 3.4 all-to-all-start.5
  206.0 3.9 all_to_all.29
  211.8 3.4 all-to-all-start.3
  216.8 4.4 %all_to_all.30 = bf16[2,1,8,16,1536]{4,3,2,1,0:T(8,128)(2,1)S(1)} all-to-all(bf16[2,1,8,16,1536]{4,3,2,1,0:T(8,128)(2,1)S(1)} %pad_maximum_fusion), channel_id=1, replica_groups=mesh['dp'=4,'segment'=2,'band'=4] {'segment'}, dimensions={0} | all-to-all | bytes 1572864 | tf_op jit(solution)/shard_map/all_to_all | solution.py:246
  228.4 25.7 %reduce-scatter.11.cloned.1.call-done = bf16[1,128,512]{2,1,0:T(8,128)(2,1)} async-done(((bf16[1,512,512]{2,1,0:T(8,128)(2,1)}), bf16[1,128,512]{2,1,0:T(8,128)(2,1)}) %reduce-scatter.11.cloned.1.call-update) | async-done | bytes 131088 | tf_op jit(solution)/shard_map/reduce_scatter | solution.py:279
  254.1 34.1 %reduce-scatter.9.cloned.1.call-done = bf16[1,128,1536]{2,1,0:T(8,128)(2,1)} async-done(((bf16[1,512,1536]{2,1,0:T(8,128)(2,1)}), bf16[1,128,1536]{2,1,0:T(8,128)(2,1)}) %reduce-scatter.9.cloned.1.call-update) | async-done | bytes 393232 | tf_op jit(solution)/shard_map/reduce_scatter | solution.py:276
  288.7 3.9 all_to_all.31
  292.7 23.1 %reduce-scatter.13.cloned.1.call-done = bf16[128,1]{1,0:T(8,128)(2,1)} async-done(((bf16[512,1]{1,0:T(8,128)(2,1)}), bf16[128,1]{1,0:T(8,128)(2,1)}) %reduce-scatter.13.cloned.1.call-update) | async-done | bytes 272
  316.6 11.8 %psum.23 = bf16[1,128]{1,0:T(2,128)(2,1)S(1)} all-reduce(bf16[1,128]{1,0:T(2,128)(2,1)S(1)} %copy.77), channel_id=1, replica_groups=mesh['dp'=4,'segment'=2,'band'=4] {'band'}, use_global_device_ids=true, to_apply=%region_28.29 | all-reduce | flops 128 | bytes 512 | tf_op jit(solution)/shard_map/psum | solution.py:290
  328.9 16.3 %all-gather.19.cloned.1.call-done = bf16[4,256,512]{2,1,0:T(8,128)(2,1)} async-done(((bf16[1,256,512]{2,1,0:T(8,128)(2,1)}), bf16[4,256,512]{2,1,0:T(8,128)(2,1)}) %all-gather.19.cloned.1.call-update) | async-done | bytes 1048592 | tf_op jit(solution)/shard_map/all_gather | solution.py:16
  347.5 38.2 %all-reduce.11.cloned.1.call-done = (bf16[1,128,1536]{2,1,0:T(8,128)(2,1)}, bf16[1,128,512]{2,1,0:T(8,128)(2,1)}) async-done(((bf16[1,128,1536]{2,1,0:T(8,128)(2,1)}, bf16[1,128,512]{2,1,0:T(8,128)(2,1)}), (bf16[1,128,1536]{2,1,0:T(8,128)(2,1)}, bf16[1,128,512]{2,1,0:T(8,128)(2,1)})) %all-reduce.11.cloned.1.call-update) | async-done | bytes 524304 | tf_op jit(solution)/shard_map/psum | solution.py:288
  (302 shorter events, 96.8 us)
Async XLA Ops:
  7.2 31.9 %all-gather.9.cloned.1.call-start = ((), (), s32[]{:S(2)}) async-start(), calls=%async_computation.11 | async-start | bytes 1310720 | tf_op jit(solution)/shard_map/all_gather | solution.py:164
  7.9 63.9 %all-gather.13.cloned.1.call-start = ((), (), s32[]{:S(2)}) async-start(), calls=%async_computation.13 | async-start | bytes 1966080 | tf_op jit(solution)/shard_map/all_gather | solution.py:165
  8.7 90.4 %all-gather.11.cloned.1.call-start = ((), (), s32[]{:S(2)}) async-start(), calls=%async_computation.12 | async-start | bytes 3145728 | tf_op jit(solution)/shard_map/all_gather | solution.py:180
  39.1 61.9 %all-gather.15.cloned.1.call-start = ((), (), s32[]{:S(2)}) async-start(), calls=%async_computation.14 | async-start | bytes 4718592 | tf_op jit(solution)/shard_map/all_gather | solution.py:181
  71.8 38.5 %all-gather.17.cloned.1.call-start = ((), (), s32[]{:S(2)}) async-start(), calls=%async_computation.15 | async-start | bytes 1572864 | tf_op jit(solution)/shard_map/all_gather | solution.py:182
  71.9 26.8 %collective-permute-start.3 = (s32[2,4,16]{2,1,0:T(4,128)S(1)}, s32[2,4,16]{2,1,0:T(4,128)S(1)}, u32[]{:S(2)}, u32[]{:S(2)}) collective-permute-start(s32[2,4,16]{2,1,0:T(4,128)S(1)} %get-tuple-element.45), channel_id=1, source_target_pairs={{1,0},{2,1},{3,2},{5,4},{6,5},{7,6},{9,8},{10,9},{11,10},{13,12},{... | collective-permute-start | bytes 1544 | tf_op jit(solution)/shard_map/ppermute | solution.py:29
  73.2 25.5 %collective-permute-start.2 = (s32[2,4,16]{2,1,0:T(4,128)S(1)}, s32[2,4,16]{2,1,0:T(4,128)S(1)}, u32[]{:S(2)}, u32[]{:S(2)}) collective-permute-start(s32[2,4,16]{2,1,0:T(4,128)S(1)} %get-tuple-element.46), channel_id=1, source_target_pairs={{0,1},{1,2},{2,3},{4,5},{5,6},{6,7},{8,9},{9,10},{10,11},{12,13},{... | collective-permute-start | bytes 1544 | tf_op jit(solution)/shard_map/ppermute | solution.py:28
  102.9 9.6 %collective-permute-start = (bf16[4,16,1024]{2,1,0:T(8,128)(2,1)S(1)}, bf16[4,16,1024]{2,1,0:T(8,128)(2,1)S(1)}, u32[]{:S(2)}, u32[]{:S(2)}) collective-permute-start(bf16[4,16,1024]{2,1,0:T(8,128)(2,1)S(1)} %get-tuple-element.34), channel_id=1, source_target_pairs={{0,1},{1,2},{2,3},{4,5},{5,6},{6,7},{8,9},{9,10},{10,11},{12,13},{... | collective-permute-start | bytes 393224 | tf_op jit(solution)/shard_map/ppermute | solution.py:28
  106.3 7.2 %collective-permute-start.1 = (bf16[4,16,1024]{2,1,0:T(8,128)(2,1)S(1)}, bf16[4,16,1024]{2,1,0:T(8,128)(2,1)S(1)}, u32[]{:S(2)}, u32[]{:S(2)}) collective-permute-start(bf16[4,16,1024]{2,1,0:T(8,128)(2,1)S(1)} %get-tuple-element.35), channel_id=1, source_target_pairs={{1,0},{2,1},{3,2},{5,4},{6,5},{7,6},{9,8},{10,9},{11,10},{13,12},{... | collective-permute-start | bytes 393224 | tf_op jit(solution)/shard_map/ppermute | solution.py:29
  123.0 69.7 %all-to-all-start.1 = ((bf16[2,1,8,16,1024]{4,3,2,1,0:T(8,128)(2,1)}), bf16[2,1,8,16,1024]{4,3,2,1,0:T(8,128)(2,1)}, u32[]{:S(2)}, u32[]{:S(2)}) async-start(bf16[2,1,8,16,1024]{4,3,2,1,0:T(8,128)(2,1)} %pad_maximum_fusion.1), calls=%async_computation.1 | async-start | bytes 1048576 | tf_op jit(solution)/shard_map/all_to_all | solution.py:243
  127.3 100.6 %reduce-scatter.7.cloned.1.call-start = ((), (), s32[]{:S(2)}) async-start(), calls=%async_computation.16 | async-start | bytes 1310720 | tf_op jit(solution)/shard_map/reduce_scatter | solution.py:273
  127.7 7.1 %collective-permute-start.4 = (bf16[4,16,1024]{2,1,0:T(8,128)(2,1)}, bf16[4,16,1024]{2,1,0:T(8,128)(2,1)S(1)}, u32[]{:S(2)}, u32[]{:S(2)}) collective-permute-start(bf16[4,16,1024]{2,1,0:T(8,128)(2,1)} %get-tuple-element.32), channel_id=1, source_target_pairs={{0,1},{1,2},{2,3},{4,5},{5,6},{6,7},{8,9},{9,10},{10,11},{12,13},{... | collective-permute-start | bytes 393224 | tf_op jit(solution)/shard_map/ppermute | solution.py:28
  131.1 7.5 %collective-permute-start.5 = (bf16[4,16,1024]{2,1,0:T(8,128)(2,1)S(1)}, bf16[4,16,1024]{2,1,0:T(8,128)(2,1)S(1)}, u32[]{:S(2)}, u32[]{:S(2)}) collective-permute-start(bf16[4,16,1024]{2,1,0:T(8,128)(2,1)S(1)} %get-tuple-element.33), channel_id=1, source_target_pairs={{1,0},{2,1},{3,2},{5,4},{6,5},{7,6},{9,8},{10,9},{11,10},{13,12},{... | collective-permute-start | bytes 393224 | tf_op jit(solution)/shard_map/ppermute | solution.py:29
  153.7 5.3 %collective-permute-start.6 = (bf16[4,16,1024]{2,1,0:T(8,128)(2,1)S(1)}, bf16[4,16,1024]{2,1,0:T(8,128)(2,1)S(1)}, u32[]{:S(2)}, u32[]{:S(2)}) collective-permute-start(bf16[4,16,1024]{2,1,0:T(8,128)(2,1)S(1)} %get-tuple-element.28), channel_id=1, source_target_pairs={{0,1},{1,2},{2,3},{4,5},{5,6},{6,7},{8,9},{9,10},{10,11},{12,13},{... | collective-permute-start | bytes 393224 | tf_op jit(solution)/shard_map/ppermute | solution.py:28
  156.5 6.9 %collective-permute-start.7 = (bf16[4,16,1024]{2,1,0:T(8,128)(2,1)S(1)}, bf16[4,16,1024]{2,1,0:T(8,128)(2,1)S(1)}, u32[]{:S(2)}, u32[]{:S(2)}) collective-permute-start(bf16[4,16,1024]{2,1,0:T(8,128)(2,1)S(1)} %get-tuple-element.29), channel_id=1, source_target_pairs={{1,0},{2,1},{3,2},{5,4},{6,5},{7,6},{9,8},{10,9},{11,10},{13,12},{... | collective-permute-start | bytes 393224 | tf_op jit(solution)/shard_map/ppermute | solution.py:29
  179.8 5.9 %collective-permute-start.8 = (bf16[4,16,1024]{2,1,0:T(8,128)(2,1)S(1)}, bf16[4,16,1024]{2,1,0:T(8,128)(2,1)S(1)}, u32[]{:S(2)}, u32[]{:S(2)}) collective-permute-start(bf16[4,16,1024]{2,1,0:T(8,128)(2,1)S(1)} %get-tuple-element.22), channel_id=1, source_target_pairs={{0,1},{1,2},{2,3},{4,5},{5,6},{6,7},{8,9},{9,10},{10,11},{12,13},{... | collective-permute-start | bytes 393224 | tf_op jit(solution)/shard_map/ppermute | solution.py:28
  183.2 6.9 %collective-permute-start.9 = (bf16[4,16,1024]{2,1,0:T(8,128)(2,1)S(1)}, bf16[4,16,1024]{2,1,0:T(8,128)(2,1)S(1)}, u32[]{:S(2)}, u32[]{:S(2)}) collective-permute-start(bf16[4,16,1024]{2,1,0:T(8,128)(2,1)S(1)} %get-tuple-element.23), channel_id=1, source_target_pairs={{1,0},{2,1},{3,2},{5,4},{6,5},{7,6},{9,8},{10,9},{11,10},{13,12},{... | collective-permute-start | bytes 393224 | tf_op jit(solution)/shard_map/ppermute | solution.py:29
  201.0 5.0 %all-to-all-start.5 = ((bf16[2,1,8,16,512]{4,3,2,1,0:T(8,128)(2,1)}), bf16[2,1,8,16,512]{4,3,2,1,0:T(8,128)(2,1)S(1)}, u32[]{:S(2)}, u32[]{:S(2)}) async-start(bf16[2,1,8,16,512]{4,3,2,1,0:T(8,128)(2,1)} %pad_maximum_fusion.13), calls=%async_computation.7 | async-start | bytes 524288 | tf_op jit(solution)/shard_map/all_to_all | solution.py:247
  204.4 49.6 %reduce-scatter.11.cloned.1.call-start = ((), (), s32[]{:S(2)}) async-start(), calls=%async_computation.18 | async-start | bytes 655360 | tf_op jit(solution)/shard_map/reduce_scatter | solution.py:279
  211.8 5.0 %all-to-all-start.3 = ((bf16[2,1,8,16,512]{4,3,2,1,0:T(8,128)(2,1)}), bf16[2,1,8,16,512]{4,3,2,1,0:T(8,128)(2,1)S(1)}, u32[]{:S(2)}, u32[]{:S(2)}) async-start(bf16[2,1,8,16,512]{4,3,2,1,0:T(8,128)(2,1)} %pad_maximum_fusion.12), calls=%async_computation.4 | async-start | bytes 524288 | tf_op jit(solution)/shard_map/all_to_all | solution.py:245
  215.2 73.0 %reduce-scatter.9.cloned.1.call-start = ((), (), s32[]{:S(2)}) async-start(), calls=%async_computation.17 | async-start | bytes 1966080 | tf_op jit(solution)/shard_map/reduce_scatter | solution.py:276
  222.9 92.8 %reduce-scatter.13.cloned.1.call-start = ((), (), s32[]{:S(2)}) async-start(), calls=%async_computation.20 | async-start | bytes 163840
  227.8 117.4 %all-gather.19.cloned.1.call-start = ((), (), s32[]{:S(2)}) async-start(), calls=%async_computation.19 | async-start | bytes 1310720 | tf_op jit(solution)/shard_map/all_gather | solution.py:16
  228.4 157.3 %all-reduce.11.cloned.1.call-start = ((), (), s32[]{:S(2)}) async-start(), calls=%async_computation.21 | async-start | bytes 1048576 | tf_op jit(solution)/shard_map/psum | solution.py:288
  (62 other events, 751.6 us)
Sparse Core Ops, SparseCore 0:
  9.9 29.2 all-gather.8
  40.9 30.8 all-gather.12
  73.4 10.5 all-gather.10
  85.4 13.2 all-gather.14
  100.1 10.1 all-gather.16
  199.4 26.0 reduce-scatter.6
  228.9 25.1 reduce-scatter.10
  257.0 31.1 reduce-scatter.8
  291.5 24.1 reduce-scatter.12
  317.1 27.9 all-gather.18
  347.6 38.0 all-reduce.10
